TPU v7x, 512 devices: a whole 4x4x16 slice. The times are simulated.
512 devices in a mesh: ep: 64 (over z, y), os: 8 (over x, core).
Axes of the slice: x: 4, y: 4, z: 16, core: 2. Of those that a mesh axis runs over, the one named last changes fastest.
Arguments:
- tokens: bfloat16 [8192, 2048], P('ep', 'os'), may hold values from -6 to 6
- cotangent: bfloat16 [8192, 2048], P('ep', 'os'), may hold values from -6 to 6
- expert_ids: int32 [8192, 8], P('ep'), may hold values from 0 to 63, all different within a row; in each aligned block of 128 rows (0 to 127, 128 to 255, ...) at most 24 rows name the same one
- route_weight: float32 [8192, 8], P('ep'), may hold values from 0.1 to 1
- placement: int32 [64], replicated, may hold values from 0 to 63, each once
- swap_flags: int32 [2, 64], replicated, may hold values from 0 to 1, as said below
- params: bfloat16 [64, 3, 2048, 384], P('ep', None, 'os'), may hold values from -1 to 1
- first_moment: bfloat16 [64, 3, 2048, 384], P('ep', None, 'os'), may hold values from -6 to 6
- second_moment: bfloat16 [64, 3, 2048, 384], P('ep', None, 'os'), may hold values from 0.5 to 20
Outputs:
- mixed: bfloat16 [8192, 2048], P('ep', 'os')
- input_grad: bfloat16 [8192, 2048], P('ep', 'os')
- new_params: bfloat16 [64, 3, 2048, 384], P('ep', None, 'os')
- new_first: bfloat16 [64, 3, 2048, 384], P('ep', None, 'os')
- new_second: bfloat16 [64, 3, 2048, 384], P('ep', None, 'os')
Inputs may be any that keep to these rules, and one draw needn't show every extreme that they name: `expert_ids`: each row names 8 different experts; in each aligned block of 128 rows (the rows of one index of ep) no expert is named by more than 24 rows, a bound that some block reaches. `placement`: A permutation of the 64 expert ids. swap_flags[r, i] = swap_flags[r, i XOR 2^b_r] with b_0 = log2(64) - 1 and b_1 = 0.
All inputs are finite; a program needn't handle non-finite values.
Results may differ from a plain program's by a relative error of at most 0.023.
Values may be sent and summed in bfloat16 or wider, within the bound.
A program may use at most 64 MiB of HBM per device.

v0:
```python
import jax
import jax.numpy as jnp
from jax import lax
from jax.sharding import PartitionSpec as P

beta_first = 0.9
beta_second = 0.999
learn_rate = 0.01
adam_eps = 1e-08
adam_count = 10.0


def from_partner(value, axis, bit):
    return lax.ppermute(value, axis, [(i, i ^ 1 << bit) for i in range(lax.axis_size(axis))])


def adam_update(weight, first, second, grad):
    first_new = beta_first * first.astype(jnp.float32) + (1.0 - beta_first) * grad
    second_new = beta_second * second.astype(jnp.float32) + (1.0 - beta_second) * grad * grad
    first_hat = first_new / (1.0 - beta_first**adam_count)
    second_hat = second_new / (1.0 - beta_second**adam_count)
    weight_new = weight.astype(jnp.float32) - learn_rate * first_hat / (
        jnp.sqrt(second_hat) + adam_eps
    )
    return (
        weight_new.astype(jnp.bfloat16),
        first_new.astype(jnp.bfloat16),
        second_new.astype(jnp.bfloat16),
    )


def derivative(back, gate, up):
    sigma = jax.nn.sigmoid(gate)
    active = gate * sigma
    d_gate = (back * up * sigma * (1.0 + gate * (1.0 - sigma))).astype(jnp.bfloat16)
    d_up = (back * active).astype(jnp.bfloat16)
    return jnp.stack((d_gate, d_up), axis=1)


def activate(gate, up):
    sigma = jax.nn.sigmoid(gate)
    return (gate * sigma * up).astype(jnp.bfloat16)


def on_device(
    tokens,
    cotangent,
    expert_ids,
    route_weight,
    placement,
    swap_flags,
    params,
    first_moment,
    second_moment,
):
    experts = lax.axis_size("ep")
    mine = lax.axis_index("ep")
    tok_rows, shard = tokens.shape
    top = expert_ids.shape[1]
    capacity = max(2, 3 * tok_rows * top // (2 * experts))
    index = jnp.arange(experts, dtype=jnp.int32)
    bits = [experts.bit_length() - 2, 0]
    place = placement
    own_flags = []
    for rnd in range(len(bits)):
        partner = index ^ 1 << bits[rnd]
        chosen = swap_flags[rnd] == 1
        place = jnp.where(chosen, place[partner], place)
        own_flags.append(jnp.sum(jnp.where(index == mine, swap_flags[rnd], 0)) == 1)
    state = jnp.stack((params, first_moment, second_moment))
    for rnd in range(len(bits)):
        moved = from_partner(state, "ep", bits[rnd])
        state = jnp.where(own_flags[rnd], moved, state)
    weight = state[0, 0]
    flat_ids = expert_ids.reshape(-1)
    match = flat_ids[:, None] == place[None, :]
    dest = jnp.sum(jnp.where(match, index[None, :], 0), axis=1)
    counts = jnp.cumsum(match.astype(jnp.int32), axis=0)
    slot = jnp.sum(jnp.where(match, counts - 1, 0), axis=1)
    position = dest * capacity + slot
    num_rows = flat_ids.shape[0]
    table = (
        jnp.zeros((experts * capacity,), jnp.int32)
        .at[position]
        .set(jnp.arange(num_rows, dtype=jnp.int32) + 1)
    )
    filled = table > 0
    source = jnp.maximum(table - 1, 0)
    owner = source // top
    weights_flat = route_weight.reshape(-1)
    x_send = jnp.where(filled[:, None], tokens[owner], jnp.zeros((), jnp.bfloat16)).reshape(
        experts, capacity, shard
    )
    dy_send = jnp.where(
        filled[:, None], weights_flat[source][:, None] * cotangent[owner].astype(jnp.float32), 0.0
    )
    dy_send = dy_send.astype(jnp.bfloat16).reshape(experts, capacity, shard)
    x_recv = lax.all_to_all(x_send, "ep", split_axis=0, concat_axis=0, tiled=True)
    x_rows = x_recv.reshape(-1, shard)
    terms = jnp.einsum("rd,kdh->rkh", x_rows, weight[:2], preferred_element_type=jnp.float32)
    summed = lax.psum(terms.astype(jnp.bfloat16), "os").astype(jnp.float32)
    gate = summed[:, 0]
    up = summed[:, 1]
    hidden = activate(gate, up)
    rows_out = jnp.einsum(
        "rh,dh->rd", hidden, weight[2], preferred_element_type=jnp.float32
    ).astype(jnp.bfloat16)
    back_y = lax.all_to_all(
        rows_out.reshape(experts, capacity, shard), "ep", split_axis=0, concat_axis=0, tiled=True
    )
    dy_recv = lax.all_to_all(dy_send, "ep", split_axis=0, concat_axis=0, tiled=True)
    dy_rows = dy_recv.reshape(-1, shard)
    back_terms = jnp.einsum("rd,dh->rh", dy_rows, weight[2], preferred_element_type=jnp.float32)
    back = lax.psum(back_terms.astype(jnp.bfloat16), "os").astype(jnp.float32)
    deriv = derivative(back, gate, up)
    grad_in = jnp.einsum("rd,rkh->kdh", x_rows, deriv, preferred_element_type=jnp.float32)
    grad_out = jnp.einsum("rd,rh->dh", dy_rows, hidden, preferred_element_type=jnp.float32)
    grad = jnp.concatenate((grad_in, grad_out[None]), axis=0)
    rows_grad = jnp.einsum(
        "rkh,kdh->rd", deriv, weight[:2], preferred_element_type=jnp.float32
    ).astype(jnp.bfloat16)
    back_dx = lax.all_to_all(
        rows_grad.reshape(experts, capacity, shard), "ep", split_axis=0, concat_axis=0, tiled=True
    )
    picked_y = back_y.reshape(-1, shard)[position].reshape(tok_rows, top, shard)
    mixed = jnp.sum(route_weight[:, :, None] * picked_y.astype(jnp.float32), axis=1).astype(
        jnp.bfloat16
    )
    picked_dx = back_dx.reshape(-1, shard)[position].reshape(tok_rows, top, shard)
    input_grad = jnp.sum(picked_dx.astype(jnp.float32), axis=1).astype(jnp.bfloat16)
    first = state[1, 0]
    second = state[2, 0]
    new_params, new_first, new_second = adam_update(weight, first, second, grad)
    return (mixed, input_grad, new_params[None], new_first[None], new_second[None])


def solution(mesh):
    placed = (
        P("ep", "os"),
        P("ep", "os"),
        P("ep", None),
        P("ep", None),
        P(),
        P(),
        P("ep", None, "os", None),
        P("ep", None, "os", None),
        P("ep", None, "os", None),
    )
    return jax.shard_map(
        on_device,
        mesh=mesh,
        in_specs=placed,
        out_specs=(
            P("ep", "os"),
            P("ep", "os"),
            P("ep", None, "os", None),
            P("ep", None, "os", None),
            P("ep", None, "os", None),
        ),
        check_vma=False,
    )
```

profile of v0, /device:TPU:1, one launch (start us, length us, event | category | flops | bytes accessed | tf_op | source)
XLA Modules:
  0.0 520.5 jit_solution(16222571462099775276)
XLA Ops:
  7.2 0.0 copy-start
  7.2 0.8 copy.18
  8.0 0.1 eq.51
  8.1 0.1 eq.45
  8.2 0.0 copy-start.14
  8.2 1.4 gather_fusion
  9.7 1.4 fusion.27
  11.1 0.8 gather_fusion.1
  11.8 0.7 compare_select_fusion.7
  12.5 0.1 compare_convert_fusion
  12.7 18.0 %reduce-window.6 = s32[64,8,128]{2,1,0:T(8,128)S(1)} reduce-window(s32[64,8,128]{2,1,0:T(8,128)S(1)} %compare_convert_fusion, s32[]{:T(128)} %constant.22.clone.1), window={size=1x1x128 pad=0_0x0_0x127_0}, to_apply=%region_1.2 | reduce-window | flops 8323072 | bytes 524292 | tf_op jit(solution)/shard_map/reduce-window
  30.7 0.1 slice.69
  30.8 0.1 copy.20
  31.0 0.1 copy.21
  31.1 0.1 add_add_fusion
  31.2 0.1 fusion.22
  31.4 4.3 scatter_custom_fusion
  35.8 0.1 copy.17
  35.9 0.1 reshape.350
  36.0 5.9 %gather_fusion.4 = f32[1536]{0:T(1024)S(1)} fusion(f32[1024]{0:T(1024)S(1)} %reshape.350, s32[2048]{0:T(1024)S(1)} %get-tuple-element.19), kind=kCustom, calls=%fused_computation.4 | custom fusion | bytes 18432 | tf_op jit(solution)/shard_map/gather | solution.py:95
  41.8 0.1 mul.168
  41.9 0.1 broadcast_in_dim.65
  42.0 4.8 gather_fusion.5
  46.8 0.0 copy-start.6
  46.8 0.0 copy-start.7
  46.8 0.0 copy-start.8
  46.8 1.3 fusion.10
  48.2 19.3 %all-to-all-start.2 = ((bf16[64,24,256]{2,1,0:T(8,128)(2,1)}), bf16[64,24,256]{2,1,0:T(8,128)(2,1)S(1)}, u32[]{:S(2)}, u32[]{:S(2)}) async-start(bf16[64,24,256]{2,1,0:T(8,128)(2,1)} %fusion.10), calls=%async_computation.2 | async-start | bytes 1572864 | tf_op jit(solution)/shard_map/all_to_all | solution.py:111
  67.5 0.0 copy-start.1
  67.5 1.4 pad_maximum_fusion.1
  68.9 11.7 %collective-permute-start = (bf16[3,1,3,256,384]{4,3,2,1,0:T(8,128)(2,1)}, bf16[3,1,3,256,384]{4,3,2,1,0:T(8,128)(2,1)}, u32[]{:S(2)}, u32[]{:S(2)}) collective-permute-start(bf16[3,1,3,256,384]{4,3,2,1,0:T(8,128)(2,1)} %pad_maximum_fusion.1), channel_id=1, source_target_pairs={{0,256},{8,264},{16,272},{24,280},{32,288},{40,296},{48,304},{56,3... | collective-permute-start | bytes 5308424 | tf_op jit(solution)/shard_map/ppermute | solution.py:14
  80.7 0.0 copy-done.1
  80.7 5.4 %gather_fusion.2 = bf16[1536,256]{1,0:T(8,128)(2,1)} fusion(bf16[128,256]{1,0:T(8,128)(2,1)S(1)} %copy-done.1, s32[2048]{0:T(1024)S(1)} %get-tuple-element.20), kind=kCustom, calls=%fused_computation.2 | custom fusion | bytes 1579008 | tf_op jit(solution)/shard_map/gather | solution.py:91
  86.0 2.3 broadcast_select_fusion.2
  88.4 17.5 %all-to-all-done.2 = bf16[64,24,256]{2,1,0:T(8,128)(2,1)S(1)} async-done(((bf16[64,24,256]{2,1,0:T(8,128)(2,1)}), bf16[64,24,256]{2,1,0:T(8,128)(2,1)S(1)}, u32[]{:S(2)}, u32[]{:S(2)}) %all-to-all-start.2) | async-done | bytes 786464 | tf_op jit(solution)/shard_map/all_to_all | solution.py:111
  105.9 14.2 %all-to-all-start = ((bf16[64,24,256]{2,1,0:T(8,128)(2,1)}), bf16[64,24,256]{2,1,0:T(8,128)(2,1)}, u32[]{:S(2)}, u32[]{:S(2)}) async-start(bf16[64,24,256]{2,1,0:T(8,128)(2,1)} %broadcast_select_fusion.2), calls=%async_computation | async-start | bytes 1572864 | tf_op jit(solution)/shard_map/all_to_all | solution.py:98
  120.1 0.0 all-reduce.3.cloned.1.call-start
  120.8 100.5 %collective-permute-done = bf16[3,1,3,256,384]{4,3,2,1,0:T(8,128)(2,1)} collective-permute-done((bf16[3,1,3,256,384]{4,3,2,1,0:T(8,128)(2,1)}, bf16[3,1,3,256,384]{4,3,2,1,0:T(8,128)(2,1)}, u32[]{:S(2)}, u32[]{:S(2)}) %collective-permute-start) | collective-permute-done | bytes 1769504 | tf_op jit(solution)/shard_map/ppermute | solution.py:14
  221.3 3.0 broadcast_select_fusion
  224.2 4.8 collective-permute-start.1
  229.7 24.4 %collective-permute-done.1 = bf16[3,1,3,256,384]{4,3,2,1,0:T(8,128)(2,1)} collective-permute-done((bf16[3,1,3,256,384]{4,3,2,1,0:T(8,128)(2,1)}, bf16[3,1,3,256,384]{4,3,2,1,0:T(8,128)(2,1)}, u32[]{:S(2)}, u32[]{:S(2)}) %collective-permute-start.1) | collective-permute-done | bytes 1769504 | tf_op jit(solution)/shard_map/ppermute | solution.py:14
  254.1 2.7 broadcast_select_fusion.1
  256.8 1.7 convolution_convert_fusion.1
  258.5 35.1 %all-to-all-done = bf16[64,24,256]{2,1,0:T(8,128)(2,1)} async-done(((bf16[64,24,256]{2,1,0:T(8,128)(2,1)}), bf16[64,24,256]{2,1,0:T(8,128)(2,1)}, u32[]{:S(2)}, u32[]{:S(2)}) %all-to-all-start) | async-done | bytes 786464 | tf_op jit(solution)/shard_map/all_to_all | solution.py:98
  293.6 3.3 convolution_convert_fusion
  296.9 0.0 all-reduce.3.cloned.1.call-update
  296.9 104.0 %all-reduce.3.cloned.1.call-done = (bf16[1536,2,384]{2,0,1:T(8,128)(2,1)}, bf16[1536,384]{1,0:T(8,128)(2,1)}) async-done(((bf16[1536,2,384]{2,0,1:T(8,128)(2,1)}, bf16[1536,384]{1,0:T(8,128)(2,1)}), (bf16[1536,2,384]{2,0,1:T(8,128)(2,1)}, bf16[1536,384]{1,0:T(8,128)(2,1)})) %all-reduce.3.cloned.1.call-update) | async-done | bytes 3538960 | tf_op jit(solution)/shard_map/psum | solution.py:101
  400.8 2.1 convert_element_type.133
  402.9 1.4 fusion.18
  404.3 0.7 copy-done.2
  405.1 1.7 fusion
  406.8 15.4 %all-to-all-start.3 = ((bf16[64,24,256]{2,1,0:T(8,128)(2,1)}), bf16[64,24,256]{2,1,0:T(8,128)(2,1)S(1)}, u32[]{:S(2)}, u32[]{:S(2)}) async-start(bf16[64,24,256]{2,1,0:T(8,128)(2,1)} %bitcast.27), calls=%async_computation.3 | async-start | bytes 1572864 | tf_op jit(solution)/shard_map/all_to_all | solution.py:122
  422.2 3.0 multiply_convert_fusion
  425.2 2.4 convolution_convert_fusion.2
  427.6 33.0 %all-to-all-done.3 = bf16[64,24,256]{2,1,0:T(8,128)(2,1)S(1)} async-done(((bf16[64,24,256]{2,1,0:T(8,128)(2,1)}), bf16[64,24,256]{2,1,0:T(8,128)(2,1)S(1)}, u32[]{:S(2)}, u32[]{:S(2)}) %all-to-all-start.3) | async-done | bytes 786464 | tf_op jit(solution)/shard_map/all_to_all | solution.py:122
  460.5 9.7 %all-to-all-start.1 = ((bf16[64,24,256]{2,1,0:T(8,128)(2,1)}), bf16[64,24,256]{2,1,0:T(8,128)(2,1)S(1)}, u32[]{:S(2)}, u32[]{:S(2)}) async-start(bf16[64,24,256]{2,1,0:T(8,128)(2,1)} %bitcast.130), calls=%async_computation.1 | async-start | bytes 1572864 | tf_op jit(solution)/shard_map/all_to_all | solution.py:108
  470.3 1.9 convolution_bitcast_fusion.1
  472.2 2.2 fusion.12
  474.4 2.1 fusion.21
  476.5 3.9 gather_fusion.6
  480.4 1.0 bitcast_reduce_fusion
  481.4 27.2 %all-to-all-done.1 = bf16[64,24,256]{2,1,0:T(8,128)(2,1)S(1)} async-done(((bf16[64,24,256]{2,1,0:T(8,128)(2,1)}), bf16[64,24,256]{2,1,0:T(8,128)(2,1)S(1)}, u32[]{:S(2)}, u32[]{:S(2)}) %all-to-all-start.1) | async-done | bytes 786464 | tf_op jit(solution)/shard_map/all_to_all | solution.py:108
  508.6 3.9 gather_fusion.3
  512.6 1.0 fusion.19
  (35 shorter events, 0.1 us)
Async XLA Ops:
  7.2 34.9 %copy-start = (bf16[128,256]{1,0:T(8,128)(2,1)S(1)}, bf16[128,256]{1,0:T(8,128)(2,1)}, u32[]{:S(2)}) copy-start(bf16[128,256]{1,0:T(8,128)(2,1)} %param.10) | copy-start | bytes 196612
  8.2 27.5 %copy-start.14 = (f32[128,8]{0,1:T(8,128)S(1)}, f32[128,8]{0,1:T(8,128)}, u32[]{:S(2)}) copy-start(f32[128,8]{0,1:T(8,128)} %param.12) | copy-start | bytes 12292
  46.8 20.6 %copy-start.6 = (bf16[1,3,256,384]{3,2,1,0:T(8,128)(2,1)S(1)}, bf16[1,3,256,384]{3,2,1,0:T(8,128)(2,1)}, u32[]{:S(2)}) copy-start(bf16[1,3,256,384]{3,2,1,0:T(8,128)(2,1)} %param.17) | copy-start | bytes 1769476
  46.8 20.6 %copy-start.7 = (bf16[1,3,256,384]{3,2,1,0:T(8,128)(2,1)S(1)}, bf16[1,3,256,384]{3,2,1,0:T(8,128)(2,1)}, u32[]{:S(2)}) copy-start(bf16[1,3,256,384]{3,2,1,0:T(8,128)(2,1)} %param.16) | copy-start | bytes 1769476
  46.8 20.6 %copy-start.8 = (bf16[1,3,256,384]{3,2,1,0:T(8,128)(2,1)S(1)}, bf16[1,3,256,384]{3,2,1,0:T(8,128)(2,1)}, u32[]{:S(2)}) copy-start(bf16[1,3,256,384]{3,2,1,0:T(8,128)(2,1)} %param.15) | copy-start | bytes 1769476
  48.2 57.7 %all-to-all-start.2 = ((bf16[64,24,256]{2,1,0:T(8,128)(2,1)}), bf16[64,24,256]{2,1,0:T(8,128)(2,1)S(1)}, u32[]{:S(2)}, u32[]{:S(2)}) async-start(bf16[64,24,256]{2,1,0:T(8,128)(2,1)} %fusion.10), calls=%async_computation.2 | async-start | bytes 1572864 | tf_op jit(solution)/shard_map/all_to_all | solution.py:111
  67.5 13.2 %copy-start.1 = (bf16[128,256]{1,0:T(8,128)(2,1)S(1)}, bf16[128,256]{1,0:T(8,128)(2,1)}, u32[]{:S(2)}) copy-start(bf16[128,256]{1,0:T(8,128)(2,1)} %param.9) | copy-start | bytes 196612
  68.9 152.3 %collective-permute-start = (bf16[3,1,3,256,384]{4,3,2,1,0:T(8,128)(2,1)}, bf16[3,1,3,256,384]{4,3,2,1,0:T(8,128)(2,1)}, u32[]{:S(2)}, u32[]{:S(2)}) collective-permute-start(bf16[3,1,3,256,384]{4,3,2,1,0:T(8,128)(2,1)} %pad_maximum_fusion.1), channel_id=1, source_target_pairs={{0,256},{8,264},{16,272},{24,280},{32,288},{40,296},{48,304},{56,3... | collective-permute-start | bytes 5308424 | tf_op jit(solution)/shard_map/ppermute | solution.py:14
  105.9 150.9 %copy-start.5 = (bf16[64,24,256]{2,1,0:T(8,128)(2,1)}, bf16[64,24,256]{2,1,0:T(8,128)(2,1)S(1)}, u32[]{:S(2)}) copy-start(bf16[64,24,256]{2,1,0:T(8,128)(2,1)S(1)} %all-to-all-done.2) | copy-start | bytes 2359300
  105.9 187.7 %all-to-all-start = ((bf16[64,24,256]{2,1,0:T(8,128)(2,1)}), bf16[64,24,256]{2,1,0:T(8,128)(2,1)}, u32[]{:S(2)}, u32[]{:S(2)}) async-start(bf16[64,24,256]{2,1,0:T(8,128)(2,1)} %broadcast_select_fusion.2), calls=%async_computation | async-start | bytes 1572864 | tf_op jit(solution)/shard_map/all_to_all | solution.py:98
  120.1 280.8 %all-reduce.3.cloned.1.call-start = ((), (), s32[]{:S(2)}) async-start(), calls=%async_computation.4 | async-start | bytes 7077888 | tf_op jit(solution)/shard_map/psum | solution.py:101
  224.2 29.9 %collective-permute-start.1 = (bf16[3,1,3,256,384]{4,3,2,1,0:T(8,128)(2,1)}, bf16[3,1,3,256,384]{4,3,2,1,0:T(8,128)(2,1)}, u32[]{:S(2)}, u32[]{:S(2)}) collective-permute-start(bf16[3,1,3,256,384]{4,3,2,1,0:T(8,128)(2,1)} %broadcast_select_fusion), channel_id=1, source_target_pairs={{0,8},{8,0},{16,24},{24,16},{32,40},{40,32},{48,56},{56,48},{64,72... | collective-permute-start | bytes 5308424 | tf_op jit(solution)/shard_map/ppermute | solution.py:14
  256.8 148.3 %copy-start.3 = (bf16[3,1,3,256,384]{4,3,2,1,0:T(8,128)(2,1)}, bf16[3,1,3,256,384]{4,3,2,1,0:T(8,128)(2,1)S(1)}, u32[]{:S(2)}) copy-start(bf16[3,1,3,256,384]{4,3,2,1,0:T(8,128)(2,1)S(1)} %broadcast_select_fusion.1) | copy-start | bytes 5308420
  400.8 2.1 copy-start.13
  402.9 2.1 copy-start.2
  405.1 1.7 copy-start.9
  405.1 1.7 copy-start.11
  406.8 53.8 %all-to-all-start.3 = ((bf16[64,24,256]{2,1,0:T(8,128)(2,1)}), bf16[64,24,256]{2,1,0:T(8,128)(2,1)S(1)}, u32[]{:S(2)}, u32[]{:S(2)}) async-start(bf16[64,24,256]{2,1,0:T(8,128)(2,1)} %bitcast.27), calls=%async_computation.3 | async-start | bytes 1572864 | tf_op jit(solution)/shard_map/all_to_all | solution.py:122
  460.5 48.1 %all-to-all-start.1 = ((bf16[64,24,256]{2,1,0:T(8,128)(2,1)}), bf16[64,24,256]{2,1,0:T(8,128)(2,1)S(1)}, u32[]{:S(2)}, u32[]{:S(2)}) async-start(bf16[64,24,256]{2,1,0:T(8,128)(2,1)} %bitcast.130), calls=%async_computation.1 | async-start | bytes 1572864 | tf_op jit(solution)/shard_map/all_to_all | solution.py:108
  470.2 1.9 copy-start.10
  470.2 1.9 copy-start.12
  472.2 2.2 copy-start.4
Sparse Core Ops, SparseCore 0:
  297.0 103.7 all-reduce.2
where the time goes:
time: 529 us; the launch traced here: 520 us
  waiting for transfers between devices  342 us (65%)
  starting transfers between devices  75.1 us (14%)
  other arithmetic  41.9 us (8%)
  local copies, waits for them, and re-layouts  32.8 us (6%)
  between operations  15.8 us (3%)
  matrix products  13.2 us (2%)
    ppermute x2, waiting for transfers between devices, from_partner(): lax.ppermute(value, axis, [(i, i ^ 1 << bit) for i in range(lax.axis_size...  125 us
    psum x1, waiting for transfers between devices, on_device(): summed = lax.psum(terms.astype(jnp.bfloat16), 'os').astype(jnp.float32)  104 us
    all_to_all x1, waiting for transfers between devices, on_device(): lax.all_to_all(x_send, 'ep', split_axis=0, concat_axis=0, tiled=True)  35.1 us
    all_to_all x1, waiting for transfers between devices, on_device(): lax.all_to_all(rows_grad.reshape(experts, capacity, shard), 'ep', split_a...  33 us
    all_to_all x1, waiting for transfers between devices, on_device(): lax.all_to_all(rows_out.reshape(experts, capacity, shard), 'ep', split_ax...  27.2 us
    all_to_all x1, starting transfers between devices, on_device(): lax.all_to_all(dy_send, 'ep', split_axis=0, concat_axis=0, tiled=True)  19.3 us
    another operation x2, other arithmetic  18 us
    all_to_all x1, waiting for transfers between devices, on_device(): lax.all_to_all(dy_send, 'ep', split_axis=0, concat_axis=0, tiled=True)  17.5 us
  transfers between devices with their start and end apart: 7, of which 7 were waited for; matrix products, arithmetic and copies ran while one was open for 6% of the time, Pallas kernels for 0%

commit v1 on v0

v1 whole, which is shorter than its diff:
```python
import functools

import jax
import jax.numpy as jnp
from jax import lax
from jax.experimental import pallas as pl
from jax.experimental.pallas import tpu as pltpu
from jax.sharding import PartitionSpec as P

MESH = pl.DeviceIdType.MESH
F32 = jnp.float32
BF16 = jnp.bfloat16

beta_first = 0.9
beta_second = 0.999
learn_rate = 0.01
adam_eps = 1e-08
adam_count = 10.0

NY = 4
NC = 2


def dot(a, b):
    return jnp.dot(a, b, preferred_element_type=F32)


def dot_nt(a, b):
    return lax.dot_general(a, b, (((1,), (1,)), ((), ())), preferred_element_type=F32)


def dot_tn(a, b):
    return lax.dot_general(a, b, (((0,), (0,)), ((), ())), preferred_element_type=F32)


def kernel(
    nz,
    nx,
    cap,
    place,
    flags,
    ids,
    rw,
    tok,
    cot,
    par,
    mom1,
    mom2,
    mixed,
    igrad,
    new_p,
    new_m,
    new_v,
    tc,
    mt,
    yb,
    zs,
    zr,
    wf,
    sx,
    rx,
    p01,
    phi,
    plo,
    psnd,
    own,
    crecv,
    xs,
    xr,
    hh,
    yo,
    yr,
    prt,
    rss,
    rsr,
    gr,
    s_loc,
    s_ag,
    s_y,
    s_z,
    s_yx,
    s_c,
    s_x,
    s_h,
    s_hc,
    s_yo,
    s_rs,
):
    ep = lax.axis_index("ep")
    osi = lax.axis_index("os")
    z, y = lax.div(ep, NY), lax.rem(ep, NY)
    x, c = lax.div(osi, NC), lax.rem(osi, NC)
    half = nz // 2
    rows_k = nz * cap
    chunk = NY * rows_k // (NC * nx)
    tok_n = tok.shape[0]
    started = []

    def dev(dz=0, dy=0, dx=0, other=False):
        e = lax.rem(z + dz + nz, nz) * NY + lax.rem(y + dy + NY, NY)
        o = lax.rem(x + dx + nx, nx) * NC + ((1 - c) if other else c)
        return (e, o)

    flip = 1 - 2 * lax.rem(y, 2)
    pair_y = (z * NY + y + flip, osi)

    def send(src, dst, sem, idx, to):
        cp = pltpu.make_async_remote_copy(
            src_ref=src,
            dst_ref=dst,
            send_sem=sem.at[(0,) + idx],
            recv_sem=sem.at[(1,) + idx],
            device_id=to,
            device_id_type=MESH,
        )
        cp.start()
        started.append(cp)
        return cp

    loc = [
        pltpu.make_async_copy(tok, tc.at[half - 1, 1, 0], s_loc.at[0]),
        pltpu.make_async_copy(cot, tc.at[half - 1, 1, 1], s_loc.at[1]),
    ]
    for cp in loc:
        cp.start()
    mt[half - 1, 1, 0:8] = ids[...].astype(F32)
    mt[half - 1, 1, 8:16] = rw[...]

    peers = [dev(dz=1), dev(dz=-1), dev(dz=half)]
    peers += [dev(dy=k) for k in range(1, NY)]
    peers += [dev(dx=m) for m in range(1, nx)]
    peers += [dev(other=True)]
    barrier = pltpu.get_barrier_semaphore()
    for d in peers:
        pl.semaphore_signal(barrier, inc=1, device_id=d, device_id_type=MESH)
    pl.semaphore_wait(barrier, len(peers))
    for cp in loc:
        cp.wait()

    ag = {}

    def ag_send(s, d):
        src = (half - 1, 1) if s == 0 else (s - 1, d)
        to = dev(dz=1 if d == 0 else -1)
        ag[s, d] = (
            send(tc.at[src], tc.at[s, d], s_ag, (0, d, s), to),
            send(mt.at[src], mt.at[s, d], s_ag, (1, d, s), to),
        )

    ag_send(0, 0)
    ag_send(0, 1)
    state = (par, mom1, mom2)
    ycp = [send(state[a], yb.at[a], s_y, (a,), pair_y) for a in range(3)]

    def held(i, iy):
        f1 = flags[1, i] == 1
        zi = lax.rem(i + half * NY, nz * NY)
        ziy = lax.rem(iy + half * NY, nz * NY)
        stay = jnp.where(flags[0, i] == 1, place[zi], place[i])
        move = jnp.where(flags[0, iy] == 1, place[ziy], place[iy])
        return jnp.where(f1, move, stay)

    experts = []
    for k in range(NY):
        yk = lax.rem(y + k, NY)
        i = z * NY + yk
        experts.append(held(i, i + 1 - 2 * lax.rem(yk, 2)).astype(F32))
    i_y = z * NY + y + flip
    i_z = lax.rem(ep + half * NY, nz * NY)
    f1_own = flags[1, ep] == 1
    f1_far = flags[1, i_z] == 1
    from_far = jnp.where(f1_own, flags[0, i_y], flags[0, ep]) == 1

    tri = (
        lax.broadcasted_iota(jnp.int32, (tok_n, tok_n), 0)
        < lax.broadcasted_iota(jnp.int32, (tok_n, tok_n), 1)
    ).astype(F32).astype(BF16)
    slots = lax.broadcasted_iota(jnp.int32, (cap, tok_n), 0).astype(F32)
    nothing = jnp.zeros((cap, tok_n), F32)

    def route(s):
        hits, weights = [], []
        for k in range(NY):
            for b in range(2):
                hit = jnp.where(mt[s, b, 0:8] == experts[k], 1.0, 0.0)
                hits.append(jnp.sum(hit, axis=0, keepdims=True))
                weights.append(jnp.sum(hit * mt[s, b, 8:16], axis=0, keepdims=True))
        mask = jnp.concatenate(hits, axis=0)
        slot = dot(mask.astype(BF16), tri)
        pick, pick_w = [], []
        for k in range(NY):
            for b in range(2):
                r = 2 * k + b
                keep = mask[r : r + 1] > 0.5
                one = jnp.where((slots == slot[r : r + 1]) & keep, 1.0, 0.0)
                w = one * weights[r]
                pick.append(jnp.concatenate((one, nothing) if b == 0 else (nothing, one), axis=1))
                pick_w.append(jnp.concatenate((w, nothing) if b == 0 else (nothing, w), axis=1))
        ones = jnp.concatenate(pick, axis=0).astype(BF16)
        wide = jnp.concatenate(pick_w, axis=0)
        high = wide.astype(BF16)
        p01[s] = ones
        phi[s] = high
        plo[s] = (wide - high.astype(F32)).astype(BF16)
        scale = jnp.sum(wide, axis=1, keepdims=True)
        t_in = jnp.concatenate((tc[s, 0, 0], tc[s, 1, 0]), axis=0)
        c_in = jnp.concatenate((tc[s, 0, 1], tc[s, 1, 1]), axis=0)
        picked = (dot(ones, t_in).astype(BF16), (scale * dot(ones, c_in)).astype(BF16))
        width = 2 * cap
        for a in range(2):
            for k in range(NY):
                part = picked[a][k * width : (k + 1) * width]
                if k == 0:
                    rx[a, 0, s * width : (s + 1) * width] = part
                else:
                    sx[a, k - 1, s * width : (s + 1) * width] = part

    for s in range(half):
        for d in range(2):
            if (s, d) not in ag:
                continue
            for cp in ag[s, d]:
                cp.wait_recv()
            if s + 1 < half - d:
                ag_send(s + 1, d)
        if s == half - 2:
            ycp[0].wait_recv()
            zs[0] = jnp.where(f1_far, yb[0], par[...])
        if s + 1 == half:
            zcp = [send(zs.at[0], zr.at[0], s_z, (0,), dev(dz=half))]
        route(s)

    rcp = {}
    for a in range(2):
        for k in range(1, NY):
            rcp[a, k] = send(sx.at[a, k - 1], rx.at[a, k], s_yx, (a, k - 1), dev(dy=k))
    for a in (1, 2):
        ycp[a].wait_recv()
        zs[a] = jnp.where(f1_far, yb[a], state[a][...])
        zcp.append(send(zs.at[a], zr.at[a], s_z, (a,), dev(dz=half)))

    for cp in rcp.values():
        cp.wait_recv()
    zcp[0].wait_recv()
    wf[...] = jnp.where(from_far, zr[0], jnp.where(f1_own, yb[0], par[...]))

    per = rows_k // chunk
    base_o, base_c = (1 - c) * (NY // NC), c * (NY // NC)
    ccp = []
    for arr in range(3):
        which = 0 if arr < 2 else 1
        for xi in range(nx):
            rows = rx[which, base_o + xi // per, (xi % per) * chunk : (xi % per + 1) * chunk]
            psnd[arr, xi] = dot(rows, wf[arr]).astype(BF16)
        ccp.append(send(psnd.at[arr], crecv.at[arr], s_c, (arr,), dev(other=True)))
    for arr in range(3):
        which = 0 if arr < 2 else 1
        for xi in range(nx):
            rows = rx[which, base_c + xi // per, (xi % per) * chunk : (xi % per + 1) * chunk]
            own[arr, xi] = dot(rows, wf[arr])
    xcp = {}
    sums = []
    for arr in range(3):
        ccp[arr].wait_recv()
        for m in range(1, nx):
            xi = lax.rem(x + m, nx)
            xs[m - 1, arr] = (own[arr, xi] + crecv[arr, xi].astype(F32)).astype(BF16)
            xcp[arr, m] = send(xs.at[m - 1, arr], xr.at[m - 1, arr], s_x, (arr, m - 1), dev(dx=m))

    def total(arr):
        acc = own[arr, x] + crecv[arr, x].astype(F32)
        for m in range(1, nx):
            xcp[arr, m].wait_recv()
            acc = acc + xr[m - 1, arr].astype(F32)
        return acc

    hcp = {}

    def spread(a):
        for m in range(1, nx):
            hcp[a, m] = send(hh.at[a, c, x], hh.at[a, c, x], s_h, (a, m - 1), dev(dx=m))
        hcp[a, 0] = send(hh.at[a, c, x], hh.at[a, c, x], s_hc, (a, 0), dev(other=True))

    own[0, x] = total(0)
    own[1, x] = total(1)
    gate, up = own[0, x], own[1, x]
    hh[0, c, x] = (gate * jax.nn.sigmoid(gate) * up).astype(BF16)
    spread(0)
    own[2, x] = total(2)
    gate, up, back = own[0, x], own[1, x], own[2, x]
    sigma = jax.nn.sigmoid(gate)
    hh[1, c, x] = (back * up * sigma * (1.0 + gate * (1.0 - sigma))).astype(BF16)
    hh[2, c, x] = (back * (gate * sigma)).astype(BF16)
    spread(1)
    spread(2)

    fcp = {}

    def forward(a):
        for m in range(1, nx):
            hcp[a, m].wait_recv()
            xi = lax.rem(x - m + nx, nx)
            fcp[a, m] = send(hh.at[a, c, xi], hh.at[a, c, xi], s_hc, (a, m), dev(other=True))

    def arrived(a):
        hcp[a, 0].wait_recv()
        for m in range(1, nx):
            fcp[a, m].wait_recv()

    bcp = {}

    def part(a, k):
        return hh[a, k // (NY // NC), (k % (NY // NC)) * per : (k % (NY // NC) + 1) * per].reshape(rows_k, -1)

    def give_back(a, k, value):
        if k == 0:
            yr[a, 0] = value
        else:
            yo[a, k - 1] = value
            bcp[a, k] = send(yo.at[a, k - 1], yr.at[a, k], s_yo, (a, k - 1), dev(dy=-k))

    forward(0)
    arrived(0)
    for k in (2, 1, 3, 0):
        give_back(0, k, dot_nt(part(0, k), wf[2]).astype(BF16))
    forward(1)
    forward(2)
    arrived(1)
    arrived(2)
    for k in (2, 1, 3, 0):
        value = dot_nt(part(1, k), wf[0]) + dot_nt(part(2, k), wf[1])
        give_back(1, k, value.astype(BF16))

    for which, a, out in ((0, 1, 0), (0, 2, 1), (1, 0, 2)):
        for k in range(NY):
            term = dot_tn(rx[which, k], part(a, k))
            gr[out] = term if k == 0 else gr[out] + term

    width = 2 * cap

    def combine(a):
        for k in range(1, NY):
            bcp[a, k].wait_recv()
        for s in range(half - 1, -1, -1):
            rows = jnp.concatenate([yr[a, k, s * width : (s + 1) * width] for k in range(NY)], axis=0)
            if a == 0:
                value = dot_tn(phi[s], rows) + dot_tn(plo[s], rows)
            else:
                value = dot_tn(p01[s], rows)
            prt[a, s, 0] = value[:tok_n]
            prt[a, s, 1] = value[tok_n:]

    combine(0)
    combine(1)
    last = {}
    for t in range(half):
        for a in range(2):
            for d in range(2):
                steps = half - d
                if t >= steps:
                    continue
                value = prt[a, steps - 1 - t, d]
                if t:
                    last[a, d].wait_recv()
                    value = value + rsr[a, d, t - 1].astype(F32)
                rss[a, d, t] = value.astype(BF16)
                last[a, d] = send(
                    rss.at[a, d, t], rsr.at[a, d, t], s_rs, (a, d, t), dev(dz=-1 if d == 0 else 1)
                )
    for a, out in ((0, mixed), (1, igrad)):
        value = prt[a, half - 1, 1]
        for d in range(2):
            last[a, d].wait_recv()
            value = value + rsr[a, d, half - d - 1].astype(F32)
        out[...] = value.astype(BF16)

    zcp[1].wait_recv()
    zcp[2].wait_recv()
    for k in range(3):
        grad = gr[k]
        first = jnp.where(from_far, zr[1, k], jnp.where(f1_own, yb[1, k], mom1[k])).astype(F32)
        second = jnp.where(from_far, zr[2, k], jnp.where(f1_own, yb[2, k], mom2[k])).astype(F32)
        first = beta_first * first + (1.0 - beta_first) * grad
        second = beta_second * second + (1.0 - beta_second) * grad * grad
        new_m[k] = first.astype(BF16)
        new_v[k] = second.astype(BF16)
        first_hat = first * (1.0 / (1.0 - beta_first**adam_count))
        second_hat = second * (1.0 / (1.0 - beta_second**adam_count))
        new_p[k] = (
            wf[k].astype(F32) - learn_rate * first_hat / (jnp.sqrt(second_hat) + adam_eps)
        ).astype(BF16)

    for cp in started:
        cp.wait_send()


def on_device(tokens, cotangent, expert_ids, route_weight, placement, swap_flags, params, first_moment, second_moment):
    nz = lax.axis_size("ep") // NY
    nx = lax.axis_size("os") // NC
    tok_n, shard = tokens.shape
    top = expert_ids.shape[1]
    _, _, _, hw = params.shape
    cap = max(2, 3 * tok_n * top // (2 * lax.axis_size("ep")))
    half = nz // 2
    rows_k = nz * cap
    chunk = NY * rows_k // (NC * nx)
    vmem = pl.BlockSpec(memory_space=pltpu.VMEM)
    smem = pl.BlockSpec(memory_space=pltpu.SMEM)
    anywhere = pl.BlockSpec(memory_space=pl.ANY)
    mat = (3, shard, hw)
    dma = pltpu.SemaphoreType.DMA
    pick = (half, NY * 2 * cap, 2 * tok_n)
    scratch = [
        pltpu.VMEM((half, 2, 2, tok_n, shard), BF16),
        pltpu.VMEM((half, 2, 2 * top, tok_n), F32),
        pltpu.VMEM((3,) + mat, BF16),
        pltpu.VMEM((3,) + mat, BF16),
        pltpu.VMEM((3,) + mat, BF16),
        pltpu.VMEM(mat, BF16),
        pltpu.VMEM((2, NY - 1, rows_k, shard), BF16),
        pltpu.VMEM((2, NY, rows_k, shard), BF16),
        pltpu.VMEM(pick, BF16),
        pltpu.VMEM(pick, BF16),
        pltpu.VMEM(pick, BF16),
        pltpu.VMEM((3, nx, chunk, hw), BF16),
        pltpu.VMEM((3, nx, chunk, hw), F32),
        pltpu.VMEM((3, nx, chunk, hw), BF16),
        pltpu.VMEM((nx - 1, 3, chunk, hw), BF16),
        pltpu.VMEM((nx - 1, 3, chunk, hw), BF16),
        pltpu.VMEM((3, NC, nx, chunk, hw), BF16),
        pltpu.VMEM((2, NY - 1, rows_k, shard), BF16),
        pltpu.VMEM((2, NY, rows_k, shard), BF16),
        pltpu.VMEM((2, half, 2, tok_n, shard), F32),
        pltpu.VMEM((2, 2, half, tok_n, shard), BF16),
        pltpu.VMEM((2, 2, half, tok_n, shard), BF16),
        pltpu.VMEM(mat, F32),
        dma((2,)),
        dma((2, 2, 2, half)),
        dma((2, 3)),
        dma((2, 3)),
        dma((2, 2, NY - 1)),
        dma((2, 3)),
        dma((2, 3, nx - 1)),
        dma((2, 3, nx - 1)),
        dma((2, 3, nx)),
        dma((2, 2, NY - 1)),
        dma((2, 2, 2, half)),
    ]
    out = pl.pallas_call(
        functools.partial(kernel, nz, nx, cap),
        name="expert_step",
        out_shape=(
            jax.ShapeDtypeStruct((tok_n, shard), BF16),
            jax.ShapeDtypeStruct((tok_n, shard), BF16),
            jax.ShapeDtypeStruct(mat, BF16),
            jax.ShapeDtypeStruct(mat, BF16),
            jax.ShapeDtypeStruct(mat, BF16),
        ),
        in_specs=[smem, smem, vmem, vmem, anywhere, anywhere, vmem, vmem, vmem],
        out_specs=(vmem,) * 5,
        scratch_shapes=scratch,
        compiler_params=pltpu.CompilerParams(
            collective_id=0, has_side_effects=True, vmem_limit_bytes=66 * 1000 * 1000
        ),
    )(
        placement,
        swap_flags,
        expert_ids.T,
        route_weight.T,
        tokens,
        cotangent,
        params[0],
        first_moment[0],
        second_moment[0],
    )
    return (out[0], out[1], out[2][None], out[3][None], out[4][None])


def solution(mesh):
    wide = P("ep", None, "os", None)
    placed = (P("ep", "os"), P("ep", "os"), P("ep", None), P("ep", None), P(), P(), wide, wide, wide)
    return jax.shard_map(
        on_device,
        mesh=mesh,
        in_specs=placed,
        out_specs=(P("ep", "os"), P("ep", "os"), wide, wide, wide),
        check_vma=False,
    )
```

time: 529 us -> 303 us (0.57); the launches traced: 520 us -> 300 us
  waiting for transfers between devices: 342 us -> 0 us
  Pallas kernels: 0 us -> 293 us
  starting transfers between devices: 75.1 us -> 0 us
  other arithmetic: 41.9 us -> 0 us
  local copies, waits for them, and re-layouts: 32.8 us -> 6.23 us
  between operations: 15.8 us -> 0.66 us
  matrix products: 13.2 us -> 0 us
    pallas_call x0 -> x1, Pallas kernels: none -> 293 us  [on_device(): pl.pallas_call(functools.partial(kernel, nz, nx, cap), name='expert_step'...]
    ppermute x2 -> x0, waiting for transfers between devices: 125 us -> none  [from_partner(): lax.ppermute(value, axis, [(i, i ^ 1 << bit) for i in range(lax.axis_size...]
    all_to_all x4 -> x0, waiting for transfers between devices: 113 us -> none  [the longest x1 35.1 us: on_device(): lax.all_to_all(x_send, 'ep', split_axis=0, concat_axis=0, tiled=True)]
    psum x1 -> x0, waiting for transfers between devices: 104 us -> none  [on_device(): summed = lax.psum(terms.astype(jnp.bfloat16), 'os').astype(jnp.float32)]
    all_to_all x4 -> x0, starting transfers between devices: 58.5 us -> none  [the longest x1 19.3 us: on_device(): lax.all_to_all(dy_send, 'ep', split_axis=0, concat_axis=0, tiled=True)]
    gather x7 -> x0, local copies, waits for them, and re-layouts: 26 us -> none  [the longest x1 5.85 us: on_device(): weights_flat[source][:, None] * cotangent[owner].astype(jnp.float32)]
    another operation x4 -> x0, other arithmetic: 20.9 us -> none
    ppermute x2 -> x0, starting transfers between devices: 16.6 us -> none  [from_partner(): lax.ppermute(value, axis, [(i, i ^ 1 << bit) for i in range(lax.axis_size...]
  transfers between devices with their start and end apart: 7 -> 0, of which waited for: 7 -> 0; matrix products, arithmetic and copies ran while one was open for 6% -> 0% of each run, Pallas kernels for 0% -> 0%
where the time goes in v1:
time: 303 us; the launch traced here: 300 us
  Pallas kernels  293 us (97%)
  local copies, waits for them, and re-layouts  6.23 us (2%)
    pallas_call x1, Pallas kernels, on_device(): pl.pallas_call(functools.partial(kernel, nz, nx, cap), name='expert_step'...  293 us
    unnamed x11, local copies, waits for them, and re-layouts  6.23 us

profile of v1, /device:TPU:1, one launch (start us, length us, event | category | flops | bytes accessed | tf_op | source)
XLA Modules:
  0.0 300.3 jit_solution(14364451595227378701)
XLA Ops:
  0.6 293.4 %expert_step.1 = (bf16[128,256]{1,0:T(8,128)(2,1)}, bf16[128,256]{1,0:T(8,128)(2,1)}, bf16[3,256,384]{2,1,0:T(8,128)(2,1)}, bf16[3,256,384]{2,1,0:T(8,128)(2,1)}, bf16[3,256,384]{2,1,0:T(8,128)(2,1)}) custom-call(s32[64]{0:T(128)} %place.1, s32[2,64]{1,0:T(2,128)} %flags.1, s32[8,128]{1,0:T(8,128)} %bitcast.14, f32[8,128]{1,0:T(8,128)} %bitcast.15, ...), custom_call_target="tpu_custom_call" | custom-call | tf_op jit(solution)/shard_map/expert_step/pallas_call | solution.py:449
  294.0 0.0 copy-start.2
  294.1 1.5 copy.19
  295.6 0.0 copy-done.2
  295.6 0.6 copy.20
  296.2 0.0 copy-start.1
  296.2 2.0 copy.21
  298.2 0.0 copy-done.1
  298.2 0.0 copy-start
  298.2 0.8 copy.22
  299.0 0.5 copy-done
  299.5 0.8 copy.23
Async XLA Ops:
  294.0 1.5 copy-start.2
  296.2 2.0 copy-start.1
  298.2 1.3 copy-start

commit v2 on v1

--- a/solution.py
+++ b/solution.py
@@ -17,6 +17,7 @@
 adam_eps = 1e-08
 adam_count = 10.0
 
+RELAY = (3, 2, 7, 2, 7, 3, 5, 2)
 NY = 4
 NC = 2
 
@@ -48,15 +49,17 @@
     mom2,
     mixed,
     igrad,
-    new_p,
-    new_m,
-    new_v,
+    grads,
+    held_p,
+    held_m,
+    held_v,
     tc,
     mt,
+    sb,
+    hop,
     yb,
     zs,
     zr,
-    wf,
     sx,
     rx,
     p01,
@@ -73,7 +76,6 @@
     prt,
     rss,
     rsr,
-    gr,
     s_loc,
     s_ag,
     s_y,
@@ -121,6 +123,8 @@
         pltpu.make_async_copy(tok, tc.at[half - 1, 1, 0], s_loc.at[0]),
         pltpu.make_async_copy(cot, tc.at[half - 1, 1, 1], s_loc.at[1]),
     ]
+    state = (par, mom1, mom2)
+    loc += [pltpu.make_async_copy(state[a], sb.at[a], s_loc.at[2 + a]) for a in range(3)]
     for cp in loc:
         cp.start()
     mt[half - 1, 1, 0:8] = ids[...].astype(F32)
@@ -134,7 +138,7 @@
     for d in peers:
         pl.semaphore_signal(barrier, inc=1, device_id=d, device_id_type=MESH)
     pl.semaphore_wait(barrier, len(peers))
-    for cp in loc:
+    for cp in loc[:3]:
         cp.wait()
 
     ag = {}
@@ -149,8 +153,11 @@
 
     ag_send(0, 0)
     ag_send(0, 1)
-    state = (par, mom1, mom2)
-    ycp = [send(state[a], yb.at[a], s_y, (a,), pair_y) for a in range(3)]
+    ycp = {(0, m): send(sb.at[0, m], yb.at[0, m], s_y, (0, m), pair_y) for m in range(3)}
+    for a in (1, 2):
+        loc[2 + a].wait()
+        for m in range(3):
+            ycp[a, m] = send(sb.at[a, m], yb.at[a, m], s_y, (a, m), pair_y)
 
     def held(i, iy):
         f1 = flags[1, i] == 1
@@ -177,6 +184,35 @@
     ).astype(F32).astype(BF16)
     slots = lax.broadcasted_iota(jnp.int32, (cap, tok_n), 0).astype(F32)
     nothing = jnp.zeros((cap, tok_n), F32)
+
+    zcp = {}
+    cut = par.shape[1] // 2
+
+    def z_hop(a, m, h):
+        if h == 0:
+            ycp[a, m].wait_recv()
+            zs[a, m] = jnp.where(f1_far, yb[a, m], sb[a, m])
+        for d in range(2):
+            piece = (a, m, pl.ds(d * cut, cut))
+            if h:
+                zcp[a, m, d, h - 1].wait_recv()
+            src = zs.at[piece] if h == 0 else hop.at[(h - 1,) + piece]
+            dst = zr.at[piece] if h == half - 1 else hop.at[(h,) + piece]
+            zcp[a, m, d, h] = send(src, dst, s_z, (a, m, d, h), dev(dz=1 if d == 0 else -1))
+
+    def z_wait(a):
+        for m in range(3):
+            for d in range(2):
+                zcp[a, m, d, half - 1].wait_recv()
+
+    def select(a, m):
+        return jnp.where(from_far, zr[a, m], jnp.where(f1_own, yb[a, m], sb[a, m]))
+
+    queue = [(a, m, h) for a in (1, 2) for h in range(half) for m in range(3)]
+
+    def relay(count):
+        for _ in range(min(count, len(queue))):
+            z_hop(*queue.pop(0))
 
     def route(s):
         hits, weights = [], []
@@ -215,7 +251,10 @@
                 else:
                     sx[a, k - 1, s * width : (s + 1) * width] = part
 
-    for s in range(half):
+    rcp = []
+    batch = 2
+    width = 2 * cap
+    for s in range(half + 1):
         for d in range(2):
             if (s, d) not in ag:
                 continue
@@ -223,26 +262,25 @@
                 cp.wait_recv()
             if s + 1 < half - d:
                 ag_send(s + 1, d)
-        if s == half - 2:
-            ycp[0].wait_recv()
-            zs[0] = jnp.where(f1_far, yb[0], par[...])
-        if s + 1 == half:
-            zcp = [send(zs.at[0], zr.at[0], s_z, (0,), dev(dz=half))]
-        route(s)
-
-    rcp = {}
-    for a in range(2):
-        for k in range(1, NY):
-            rcp[a, k] = send(sx.at[a, k - 1], rx.at[a, k], s_yx, (a, k - 1), dev(dy=k))
-    for a in (1, 2):
-        ycp[a].wait_recv()
-        zs[a] = jnp.where(f1_far, yb[a], state[a][...])
-        zcp.append(send(zs.at[a], zr.at[a], s_z, (a,), dev(dz=half)))
-
-    for cp in rcp.values():
+        if s > 0:
+            for m in range(3):
+                z_hop(0, m, s - 1)
+        if s < half:
+            route(s)
+            if s % batch == batch - 1:
+                b = s // batch
+                piece = pl.ds(b * batch * width, batch * width)
+                for a in range(2):
+                    for k in range(1, NY):
+                        rcp.append(
+                            send(sx.at[a, k - 1, piece], rx.at[a, k, piece], s_yx, (a, k - 1, b), dev(dy=k))
+                        )
+    relay(RELAY[0])
+    for cp in rcp:
         cp.wait_recv()
-    zcp[0].wait_recv()
-    wf[...] = jnp.where(from_far, zr[0], jnp.where(f1_own, yb[0], par[...]))
+    z_wait(0)
+    for m in range(3):
+        held_p[m] = select(0, m)
 
     per = rows_k // chunk
     base_o, base_c = (1 - c) * (NY // NC), c * (NY // NC)
@@ -251,13 +289,14 @@
         which = 0 if arr < 2 else 1
         for xi in range(nx):
             rows = rx[which, base_o + xi // per, (xi % per) * chunk : (xi % per + 1) * chunk]
-            psnd[arr, xi] = dot(rows, wf[arr]).astype(BF16)
+            psnd[arr, xi] = dot(rows, held_p[arr]).astype(BF16)
         ccp.append(send(psnd.at[arr], crecv.at[arr], s_c, (arr,), dev(other=True)))
+    relay(RELAY[1])
     for arr in range(3):
         which = 0 if arr < 2 else 1
         for xi in range(nx):
             rows = rx[which, base_c + xi // per, (xi % per) * chunk : (xi % per + 1) * chunk]
-            own[arr, xi] = dot(rows, wf[arr])
+            own[arr, xi] = dot(rows, held_p[arr])
     xcp = {}
     sums = []
     for arr in range(3):
@@ -267,6 +306,8 @@
             xs[m - 1, arr] = (own[arr, xi] + crecv[arr, xi].astype(F32)).astype(BF16)
             xcp[arr, m] = send(xs.at[m - 1, arr], xr.at[m - 1, arr], s_x, (arr, m - 1), dev(dx=m))
 
+    relay(RELAY[2])
+
     def total(arr):
         acc = own[arr, x] + crecv[arr, x].astype(F32)
         for m in range(1, nx):
@@ -286,6 +327,7 @@
     gate, up = own[0, x], own[1, x]
     hh[0, c, x] = (gate * jax.nn.sigmoid(gate) * up).astype(BF16)
     spread(0)
+    relay(RELAY[3])
     own[2, x] = total(2)
     gate, up, back = own[0, x], own[1, x], own[2, x]
     sigma = jax.nn.sigmoid(gate)
@@ -294,6 +336,7 @@
     spread(1)
     spread(2)
 
+    relay(RELAY[4])
     fcp = {}
 
     def forward(a):
@@ -322,22 +365,22 @@
     forward(0)
     arrived(0)
     for k in (2, 1, 3, 0):
-        give_back(0, k, dot_nt(part(0, k), wf[2]).astype(BF16))
+        give_back(0, k, dot_nt(part(0, k), held_p[2]).astype(BF16))
+    relay(RELAY[5])
     forward(1)
     forward(2)
     arrived(1)
     arrived(2)
     for k in (2, 1, 3, 0):
-        value = dot_nt(part(1, k), wf[0]) + dot_nt(part(2, k), wf[1])
+        value = dot_nt(part(1, k), held_p[0]) + dot_nt(part(2, k), held_p[1])
         give_back(1, k, value.astype(BF16))
 
     for which, a, out in ((0, 1, 0), (0, 2, 1), (1, 0, 2)):
         for k in range(NY):
             term = dot_tn(rx[which, k], part(a, k))
-            gr[out] = term if k == 0 else gr[out] + term
-
-    width = 2 * cap
-
+            grads[out] = term if k == 0 else grads[out] + term
+
+    relay(RELAY[6])
     def combine(a):
         for k in range(1, NY):
             bcp[a, k].wait_recv()
@@ -367,6 +410,8 @@
                 last[a, d] = send(
                     rss.at[a, d, t], rsr.at[a, d, t], s_rs, (a, d, t), dev(dz=-1 if d == 0 else 1)
                 )
+        relay(RELAY[7])
+    relay(len(queue))
     for a, out in ((0, mixed), (1, igrad)):
         value = prt[a, half - 1, 1]
         for d in range(2):
@@ -374,24 +419,22 @@
             value = value + rsr[a, d, half - d - 1].astype(F32)
         out[...] = value.astype(BF16)
 
-    zcp[1].wait_recv()
-    zcp[2].wait_recv()
-    for k in range(3):
-        grad = gr[k]
-        first = jnp.where(from_far, zr[1, k], jnp.where(f1_own, yb[1, k], mom1[k])).astype(F32)
-        second = jnp.where(from_far, zr[2, k], jnp.where(f1_own, yb[2, k], mom2[k])).astype(F32)
-        first = beta_first * first + (1.0 - beta_first) * grad
-        second = beta_second * second + (1.0 - beta_second) * grad * grad
-        new_m[k] = first.astype(BF16)
-        new_v[k] = second.astype(BF16)
-        first_hat = first * (1.0 / (1.0 - beta_first**adam_count))
-        second_hat = second * (1.0 / (1.0 - beta_second**adam_count))
-        new_p[k] = (
-            wf[k].astype(F32) - learn_rate * first_hat / (jnp.sqrt(second_hat) + adam_eps)
-        ).astype(BF16)
+    for a, out in ((1, held_m), (2, held_v)):
+        z_wait(a)
+        for m in range(3):
+            out[m] = select(a, m)
 
     for cp in started:
         cp.wait_send()
+
+
+def adam_update(weight, first, second, grad):
+    first_new = beta_first * first.astype(F32) + (1.0 - beta_first) * grad
+    second_new = beta_second * second.astype(F32) + (1.0 - beta_second) * grad * grad
+    first_hat = first_new / (1.0 - beta_first**adam_count)
+    second_hat = second_new / (1.0 - beta_second**adam_count)
+    weight_new = weight.astype(F32) - learn_rate * first_hat / (jnp.sqrt(second_hat) + adam_eps)
+    return weight_new.astype(BF16), first_new.astype(BF16), second_new.astype(BF16)
 
 
 def on_device(tokens, cotangent, expert_ids, route_weight, placement, swap_flags, params, first_moment, second_moment):
@@ -414,9 +457,10 @@
         pltpu.VMEM((half, 2, 2, tok_n, shard), BF16),
         pltpu.VMEM((half, 2, 2 * top, tok_n), F32),
         pltpu.VMEM((3,) + mat, BF16),
+        pltpu.VMEM((half - 1, 3) + mat, BF16),
         pltpu.VMEM((3,) + mat, BF16),
         pltpu.VMEM((3,) + mat, BF16),
-        pltpu.VMEM(mat, BF16),
+        pltpu.VMEM((3,) + mat, BF16),
         pltpu.VMEM((2, NY - 1, rows_k, shard), BF16),
         pltpu.VMEM((2, NY, rows_k, shard), BF16),
         pltpu.VMEM(pick, BF16),
@@ -433,12 +477,11 @@
         pltpu.VMEM((2, half, 2, tok_n, shard), F32),
         pltpu.VMEM((2, 2, half, tok_n, shard), BF16),
         pltpu.VMEM((2, 2, half, tok_n, shard), BF16),
-        pltpu.VMEM(mat, F32),
-        dma((2,)),
+        dma((5,)),
         dma((2, 2, 2, half)),
-        dma((2, 3)),
-        dma((2, 3)),
-        dma((2, 2, NY - 1)),
+        dma((2, 3, 3)),
+        dma((2, 3, 3, 2, half)),
+        dma((2, 2, NY - 1, half // 2)),
         dma((2, 3)),
         dma((2, 3, nx - 1)),
         dma((2, 3, nx - 1)),
@@ -452,12 +495,13 @@
         out_shape=(
             jax.ShapeDtypeStruct((tok_n, shard), BF16),
             jax.ShapeDtypeStruct((tok_n, shard), BF16),
+            jax.ShapeDtypeStruct(mat, F32),
             jax.ShapeDtypeStruct(mat, BF16),
             jax.ShapeDtypeStruct(mat, BF16),
             jax.ShapeDtypeStruct(mat, BF16),
         ),
-        in_specs=[smem, smem, vmem, vmem, anywhere, anywhere, vmem, vmem, vmem],
-        out_specs=(vmem,) * 5,
+        in_specs=[smem, smem, vmem, vmem] + [anywhere] * 5,
+        out_specs=(vmem,) * 6,
         scratch_shapes=scratch,
         compiler_params=pltpu.CompilerParams(
             collective_id=0, has_side_effects=True, vmem_limit_bytes=66 * 1000 * 1000
@@ -473,7 +517,9 @@
         first_moment[0],
         second_moment[0],
     )
-    return (out[0], out[1], out[2][None], out[3][None], out[4][None])
+    mixed, input_grad, grad, *held = out
+    updated = adam_update(*held, grad)
+    return (mixed, input_grad, *(a[None] for a in updated))
 
 
 def solution(mesh):

time: 303 us -> 234 us (0.77)
  Pallas kernels: 293 us -> 227 us
  local copies, waits for them, and re-layouts: 6.23 us -> 1.27 us
  other arithmetic: 0 us -> 4.33 us
    pallas_call x1, Pallas kernels: 293 us -> 227 us  [on_device(): pl.pallas_call(functools.partial(kernel, nz, nx, cap), name='expert_step'...]
    unnamed x11 -> x6, local copies, waits for them, and re-layouts: 6.23 us -> 1.27 us
    broadcast_in_dim x0 -> x1, other arithmetic: none -> 4.33 us  [on_device(): return (mixed, input_grad, *(a[None] for a in updated))]
where the time goes in v2:
time: 234 us
  Pallas kernels  227 us (97%)
  other arithmetic  4.33 us (2%)
    pallas_call x1, Pallas kernels, on_device(): pl.pallas_call(functools.partial(kernel, nz, nx, cap), name='expert_step'...  227 us

profile of v2, /device:TPU:1, one launch (start us, length us, event | category | flops | bytes accessed | tf_op | source)
XLA Modules:
  0.0 233.5 jit_solution(14496827578760448719)
XLA Ops:
  0.6 227.3 %expert_step.1 = (bf16[128,256]{1,0:T(8,128)(2,1)}, bf16[128,256]{1,0:T(8,128)(2,1)}, f32[3,256,384]{2,1,0:T(8,128)}, bf16[3,256,384]{2,1,0:T(8,128)(2,1)}, bf16...) custom-call(s32[64]{0:T(128)} %place.1, s32[2,64]{1,0:T(2,128)} %flags.1, s32[8,128]{1,0:T(8,128)} %bitcast.14, ...), custom_call_target="tpu_custom_call" | custom-call | tf_op jit(solution)/shard_map/expert_step/pallas_call | solution.py:492
  227.9 0.0 copy-start.1
  227.9 0.0 copy-start
  227.9 4.3 %fusion.3 = (bf16[1,3,256,384]{3,2,1,0:T(8,128)(2,1)}, bf16[1,3,256,384]{3,2,1,0:T(8,128)(2,1)}, bf16[1,3,256,384]{3,2,1,0:T(8,128)(2,1)}) fusion(f32[3,256,384]{2,1,0:T(8,128)} %get-tuple-element.15, bf16[3,256,384]{2,1,0:T(8,128)(2,1)} %get-tuple-element.16, bf16[3,256,384]{2,1,0:T(8,128)(2,1)} %get-tuple-element.14, bf16[3,256,384]{2,1,0:T(8,128)(2,1)} %get-tuple-element.13), kind=kLoop, calls=%fused_computation.6 | loop fusion | flops 5308416 | bytes 4718592 | tf_op jit(solution)/shard_map/broadcast_in_dim | solution.py:522
  232.3 0.0 copy-done.1
  232.3 0.6 copy.16
  232.9 0.0 copy-done
  232.9 0.6 copy.17
Async XLA Ops:
  227.9 4.4 %copy-start.1 = (bf16[128,256]{1,0:T(8,128)(2,1)S(1)}, bf16[128,256]{1,0:T(8,128)(2,1)}, u32[]{:S(2)}) copy-start(bf16[128,256]{1,0:T(8,128)(2,1)} %get-tuple-element.25) | copy-start | bytes 196612
  227.9 5.0 %copy-start = (bf16[128,256]{1,0:T(8,128)(2,1)S(1)}, bf16[128,256]{1,0:T(8,128)(2,1)}, u32[]{:S(2)}) copy-start(bf16[128,256]{1,0:T(8,128)(2,1)} %get-tuple-element.26) | copy-start | bytes 196612

commit v3 on v2

--- a/solution.py
+++ b/solution.py
@@ -17,7 +17,7 @@
 adam_eps = 1e-08
 adam_count = 10.0
 
-RELAY = (3, 2, 7, 2, 7, 3, 5, 2)
+RELAY = (4, 2, 8, 3, 8, 3, 5, 2)
 NY = 4
 NC = 2
 
@@ -130,7 +130,7 @@
     mt[half - 1, 1, 0:8] = ids[...].astype(F32)
     mt[half - 1, 1, 8:16] = rw[...]
 
-    peers = [dev(dz=1), dev(dz=-1), dev(dz=half)]
+    peers = [dev(dz=1), dev(dz=-1)]
     peers += [dev(dy=k) for k in range(1, NY)]
     peers += [dev(dx=m) for m in range(1, nx)]
     peers += [dev(other=True)]
@@ -143,16 +143,17 @@
 
     ag = {}
 
-    def ag_send(s, d):
+    def ag_send(s, d, part):
         src = (half - 1, 1) if s == 0 else (s - 1, d)
-        to = dev(dz=1 if d == 0 else -1)
-        ag[s, d] = (
-            send(tc.at[src], tc.at[s, d], s_ag, (0, d, s), to),
-            send(mt.at[src], mt.at[s, d], s_ag, (1, d, s), to),
+        ref, tail = (tc, (part,)) if part < 2 else (mt, ())
+        ag[s, d, part] = send(
+            ref.at[src + tail], ref.at[(s, d) + tail], s_ag, (part, d, s), dev(dz=1 if d == 0 else -1)
         )
 
-    ag_send(0, 0)
-    ag_send(0, 1)
+    parts = (0, 2, 1)
+    for part in parts:
+        for d in range(2):
+            ag_send(0, d, part)
     ycp = {(0, m): send(sb.at[0, m], yb.at[0, m], s_y, (0, m), pair_y) for m in range(3)}
     for a in (1, 2):
         loc[2 + a].wait()
@@ -255,13 +256,13 @@
     batch = 2
     width = 2 * cap
     for s in range(half + 1):
-        for d in range(2):
-            if (s, d) not in ag:
-                continue
-            for cp in ag[s, d]:
-                cp.wait_recv()
-            if s + 1 < half - d:
-                ag_send(s + 1, d)
+        for part in parts:
+            for d in range(2):
+                if (s, d, part) not in ag:
+                    continue
+                ag[s, d, part].wait_recv()
+                if s + 1 < half - d:
+                    ag_send(s + 1, d, part)
         if s > 0:
             for m in range(3):
                 z_hop(0, m, s - 1)
@@ -428,13 +429,24 @@
         cp.wait_send()
 
 
-def adam_update(weight, first, second, grad):
-    first_new = beta_first * first.astype(F32) + (1.0 - beta_first) * grad
-    second_new = beta_second * second.astype(F32) + (1.0 - beta_second) * grad * grad
-    first_hat = first_new / (1.0 - beta_first**adam_count)
-    second_hat = second_new / (1.0 - beta_second**adam_count)
-    weight_new = weight.astype(F32) - learn_rate * first_hat / (jnp.sqrt(second_hat) + adam_eps)
-    return weight_new.astype(BF16), first_new.astype(BF16), second_new.astype(BF16)
+def adam(grad, weight, first, second, mixed_in, input_in, new_p, new_m, new_v, mixed, igrad):
+    @pl.when(pl.program_id(0) == 0)
+    def _():
+        mixed[...] = mixed_in[...]
+        igrad[...] = input_in[...]
+
+    g = grad[...]
+    m = beta_first * first[...].astype(F32) + (1.0 - beta_first) * g
+    v = beta_second * second[...].astype(F32) + (1.0 - beta_second) * g * g
+    new_m[...] = m.astype(BF16)
+    new_v[...] = v.astype(BF16)
+    first_hat = m * (1.0 / (1.0 - beta_first**adam_count))
+    second_hat = v * (1.0 / (1.0 - beta_second**adam_count))
+    step = learn_rate * first_hat / (jnp.sqrt(second_hat) + adam_eps)
+    new_p[...] = (weight[...].astype(F32) - step).astype(BF16)
+
+
+ADAM_CUT = 1
 
 
 def on_device(tokens, cotangent, expert_ids, route_weight, placement, swap_flags, params, first_moment, second_moment):
@@ -478,7 +490,7 @@
         pltpu.VMEM((2, 2, half, tok_n, shard), BF16),
         pltpu.VMEM((2, 2, half, tok_n, shard), BF16),
         dma((5,)),
-        dma((2, 2, 2, half)),
+        dma((2, 3, 2, half)),
         dma((2, 3, 3)),
         dma((2, 3, 3, 2, half)),
         dma((2, 2, NY - 1, half // 2)),
@@ -518,7 +530,17 @@
         second_moment[0],
     )
     mixed, input_grad, grad, *held = out
-    updated = adam_update(*held, grad)
+    tile = pl.BlockSpec((1, shard // ADAM_CUT, hw), lambda i: (i // ADAM_CUT, i % ADAM_CUT, 0))
+    whole = pl.BlockSpec((tok_n, shard), lambda i: (0, 0))
+    rows_shape = jax.ShapeDtypeStruct((tok_n, shard), BF16)
+    *updated, mixed, input_grad = pl.pallas_call(
+        adam,
+        name="adam",
+        grid=(3 * ADAM_CUT,),
+        in_specs=[tile] * 4 + [whole] * 2,
+        out_specs=[tile] * 3 + [whole] * 2,
+        out_shape=[jax.ShapeDtypeStruct(mat, BF16)] * 3 + [rows_shape] * 2,
+    )(grad, *held, mixed, input_grad)
     return (mixed, input_grad, *(a[None] for a in updated))
 
 

time: 234 us -> 228 us (0.974)
  other arithmetic: 4.33 us -> 0 us
    pallas_call x1, Pallas kernels: 227 us -> 223 us  [on_device(): pl.pallas_call(functools.partial(kernel, nz, nx, cap), name='expert_step'...]
    broadcast_in_dim x1 -> x0, other arithmetic: 4.33 us -> none  [on_device(): return (mixed, input_grad, *(a[None] for a in updated))]
    pallas_call x0 -> x1, Pallas kernels: none -> 4.3 us  [on_device(): pl.pallas_call(adam, name='adam', grid=(3 * ADAM_CUT,), in_specs=[tile] *...]
where the time goes in v3:
time: 228 us
  Pallas kernels  227 us (100%)
    pallas_call x1, Pallas kernels, on_device(): pl.pallas_call(functools.partial(kernel, nz, nx, cap), name='expert_step'...  223 us

profile of v3, /device:TPU:1, one launch (start us, length us, event | category | flops | bytes accessed | tf_op | source)
XLA Modules:
  0.0 227.5 jit_solution(10846908051974674367)
XLA Ops:
  0.6 222.6 %expert_step.1 = (bf16[128,256]{1,0:T(8,128)(2,1)}, bf16[128,256]{1,0:T(8,128)(2,1)}, f32[3,256,384]{2,1,0:T(8,128)}, bf16[3,256,384]{2,1,0:T(8,128)(2,1)}, bf16...) custom-call(s32[64]{0:T(128)} %place.1, s32[2,64]{1,0:T(2,128)} %flags.1, s32[8,128]{1,0:T(8,128)} %bitcast.11, ...), custom_call_target="tpu_custom_call" | custom-call | tf_op jit(solution)/shard_map/expert_step/pallas_call | solution.py:504
  223.2 4.3 %adam.1 = (bf16[3,256,384]{2,1,0:T(8,128)(2,1)}, bf16[3,256,384]{2,1,0:T(8,128)(2,1)}, bf16[3,256,384]{2,1,0:T(8,128)(2,1)}, bf16[128,256]{1,0:T(8,128)(2,1)}, bf16[128,256]{1,0:T(8,128)(2,1)}) custom-call(f32[3,256,384]{2,1,0:T(8,128)} %get-tuple-element.16.grad, bf16[3,256,384]{2,1,0:T(8,128)(2,1)} %get-tuple-element.17.weight, ...), custom_call_target="tpu_custom_call" | custom-call | tf_op jit(solution)/shard_map/adam/pallas_call | solution.py:536

commit v4 on v3

--- a/solution.py
+++ b/solution.py
@@ -49,10 +49,12 @@
     mom2,
     mixed,
     igrad,
+    new_p,
+    new_m,
+    new_v,
     grads,
+    scale_p,
     held_p,
-    held_m,
-    held_v,
     tc,
     mt,
     sb,
@@ -155,7 +157,7 @@
         for d in range(2):
             ag_send(0, d, part)
     ycp = {(0, m): send(sb.at[0, m], yb.at[0, m], s_y, (0, m), pair_y) for m in range(3)}
-    for a in (1, 2):
+    for a in (2, 1):
         loc[2 + a].wait()
         for m in range(3):
             ycp[a, m] = send(sb.at[a, m], yb.at[a, m], s_y, (a, m), pair_y)
@@ -201,15 +203,14 @@
             dst = zr.at[piece] if h == half - 1 else hop.at[(h,) + piece]
             zcp[a, m, d, h] = send(src, dst, s_z, (a, m, d, h), dev(dz=1 if d == 0 else -1))
 
-    def z_wait(a):
-        for m in range(3):
-            for d in range(2):
-                zcp[a, m, d, half - 1].wait_recv()
+    def z_wait(a, m):
+        for d in range(2):
+            zcp[a, m, d, half - 1].wait_recv()
 
     def select(a, m):
         return jnp.where(from_far, zr[a, m], jnp.where(f1_own, yb[a, m], sb[a, m]))
 
-    queue = [(a, m, h) for a in (1, 2) for h in range(half) for m in range(3)]
+    queue = [(a, m, h) for a in (2, 1) for h in range(half) for m in range(3)]
 
     def relay(count):
         for _ in range(min(count, len(queue))):
@@ -279,8 +280,8 @@
     relay(RELAY[0])
     for cp in rcp:
         cp.wait_recv()
-    z_wait(0)
     for m in range(3):
+        z_wait(0, m)
         held_p[m] = select(0, m)
 
     per = rows_k // chunk
@@ -396,6 +397,20 @@
 
     combine(0)
     combine(1)
+    def second_moment(k):
+        z_wait(2, k)
+        grad = grads[k]
+        v = beta_second * select(2, k).astype(F32) + (1.0 - beta_second) * grad * grad
+        new_v[k] = v.astype(BF16)
+        root = jnp.sqrt(v * (1.0 / (1.0 - beta_second**adam_count)))
+        scale_p[k] = (learn_rate / (1.0 - beta_first**adam_count)) / (root + adam_eps)
+
+    def first_moment(k):
+        z_wait(1, k)
+        m = beta_first * select(1, k).astype(F32) + (1.0 - beta_first) * grads[k]
+        new_m[k] = m.astype(BF16)
+        new_p[k] = (held_p[k].astype(F32) - m * scale_p[k]).astype(BF16)
+
     last = {}
     for t in range(half):
         for a in range(2):
@@ -412,7 +427,11 @@
                     rss.at[a, d, t], rsr.at[a, d, t], s_rs, (a, d, t), dev(dz=-1 if d == 0 else 1)
                 )
         relay(RELAY[7])
+        if t < 3:
+            second_moment(t)
     relay(len(queue))
+    first_moment(0)
+    first_moment(1)
     for a, out in ((0, mixed), (1, igrad)):
         value = prt[a, half - 1, 1]
         for d in range(2):
@@ -420,33 +439,24 @@
             value = value + rsr[a, d, half - d - 1].astype(F32)
         out[...] = value.astype(BF16)
 
-    for a, out in ((1, held_m), (2, held_v)):
-        z_wait(a)
-        for m in range(3):
-            out[m] = select(a, m)
+    first_moment(2)
 
     for cp in started:
         cp.wait_send()
 
 
-def adam(grad, weight, first, second, mixed_in, input_in, new_p, new_m, new_v, mixed, igrad):
-    @pl.when(pl.program_id(0) == 0)
-    def _():
-        mixed[...] = mixed_in[...]
-        igrad[...] = input_in[...]
-
-    g = grad[...]
-    m = beta_first * first[...].astype(F32) + (1.0 - beta_first) * g
-    v = beta_second * second[...].astype(F32) + (1.0 - beta_second) * g * g
-    new_m[...] = m.astype(BF16)
-    new_v[...] = v.astype(BF16)
-    first_hat = m * (1.0 / (1.0 - beta_first**adam_count))
-    second_hat = v * (1.0 / (1.0 - beta_second**adam_count))
-    step = learn_rate * first_hat / (jnp.sqrt(second_hat) + adam_eps)
-    new_p[...] = (weight[...].astype(F32) - step).astype(BF16)
-
-
-ADAM_CUT = 1
+def hand_over(*refs):
+    n = (len(refs) - 1) // 3
+    src, dst, held, sem = refs[:n], refs[n : 2 * n], refs[2 * n : 3 * n], refs[-1]
+    into = [pltpu.make_async_copy(src[i], held[i], sem.at[0, i]) for i in range(n)]
+    out = [pltpu.make_async_copy(held[i], dst[i], sem.at[1, i]) for i in range(n)]
+    for cp in into:
+        cp.start()
+    for i in range(n):
+        into[i].wait()
+        out[i].start()
+    for cp in out:
+        cp.wait()
 
 
 def on_device(tokens, cotangent, expert_ids, route_weight, placement, swap_flags, params, first_moment, second_moment):
@@ -466,6 +476,9 @@
     dma = pltpu.SemaphoreType.DMA
     pick = (half, NY * 2 * cap, 2 * tok_n)
     scratch = [
+        pltpu.VMEM(mat, F32),
+        pltpu.VMEM(mat, F32),
+        pltpu.VMEM(mat, BF16),
         pltpu.VMEM((half, 2, 2, tok_n, shard), BF16),
         pltpu.VMEM((half, 2, 2 * top, tok_n), F32),
         pltpu.VMEM((3,) + mat, BF16),
@@ -507,13 +520,12 @@
         out_shape=(
             jax.ShapeDtypeStruct((tok_n, shard), BF16),
             jax.ShapeDtypeStruct((tok_n, shard), BF16),
-            jax.ShapeDtypeStruct(mat, F32),
             jax.ShapeDtypeStruct(mat, BF16),
             jax.ShapeDtypeStruct(mat, BF16),
             jax.ShapeDtypeStruct(mat, BF16),
         ),
         in_specs=[smem, smem, vmem, vmem] + [anywhere] * 5,
-        out_specs=(vmem,) * 6,
+        out_specs=(vmem,) * 5,
         scratch_shapes=scratch,
         compiler_params=pltpu.CompilerParams(
             collective_id=0, has_side_effects=True, vmem_limit_bytes=66 * 1000 * 1000
@@ -529,18 +541,15 @@
         first_moment[0],
         second_moment[0],
     )
-    mixed, input_grad, grad, *held = out
-    tile = pl.BlockSpec((1, shard // ADAM_CUT, hw), lambda i: (i // ADAM_CUT, i % ADAM_CUT, 0))
-    whole = pl.BlockSpec((tok_n, shard), lambda i: (0, 0))
-    rows_shape = jax.ShapeDtypeStruct((tok_n, shard), BF16)
-    *updated, mixed, input_grad = pl.pallas_call(
-        adam,
-        name="adam",
-        grid=(3 * ADAM_CUT,),
-        in_specs=[tile] * 4 + [whole] * 2,
-        out_specs=[tile] * 3 + [whole] * 2,
-        out_shape=[jax.ShapeDtypeStruct(mat, BF16)] * 3 + [rows_shape] * 2,
-    )(grad, *held, mixed, input_grad)
+    shapes = [jax.ShapeDtypeStruct(a.shape, BF16) for a in out]
+    mixed, input_grad, *updated = pl.pallas_call(
+        hand_over,
+        name="hand_over",
+        in_specs=[anywhere] * 5,
+        out_specs=[anywhere] * 5,
+        out_shape=shapes,
+        scratch_shapes=[pltpu.VMEM(a.shape, BF16) for a in shapes] + [dma((2, 5))],
+    )(*out)
     return (mixed, input_grad, *(a[None] for a in updated))
 
 

time: 228 us -> 226 us (level)
  no operation moved by 1% of the time
where the time goes in v4:
time: 226 us; the launch traced here: 225 us
  Pallas kernels  225 us (100%)
    pallas_call x1, Pallas kernels, on_device(): pl.pallas_call(functools.partial(kernel, nz, nx, cap), name='expert_step'...  222 us

profile of v4, /device:TPU:1, one launch (start us, length us, event | category | flops | bytes accessed | tf_op | source)
XLA Modules:
  0.0 225.3 jit_solution(890496378714992627)
XLA Ops:
  0.6 222.3 %expert_step.1 = (bf16[128,256]{1,0:T(8,128)(2,1)}, bf16[128,256]{1,0:T(8,128)(2,1)}, bf16[3,256,384]{2,1,0:T(8,128)(2,1)}, bf16[3,256,384]{2,1,0:T(8,128)(2,1)}, bf16[3,256,384]{2,1,0:T(8,128)(2,1)}) custom-call(s32[64]{0:T(128)} %place.1, s32[2,64]{1,0:T(2,128)} %flags.1, s32[8,128]{1,0:T(8,128)} %bitcast.11, f32[8,128]{1,0:T(8,128)} %bitcast.12, ...), custom_call_target="tpu_custom_call" | custom-call | tf_op jit(solution)/shard_map/expert_step/pallas_call | solution.py:517
  222.9 2.4 %hand_over.1 = (bf16[128,256]{1,0:T(8,128)(2,1)}, bf16[128,256]{1,0:T(8,128)(2,1)}, bf16[3,256,384]{2,1,0:T(8,128)(2,1)}, bf16[3,256,384]{2,1,0:T(8,128)(2,1)}, bf16[3,256,384]{2,1,0:T(8,128)(2,1)}) custom-call(bf16[128,256]{1,0:T(8,128)(2,1)} %get-tuple-element.15.refs_0_, bf16[128,256]{1,0:T(8,128)(2,1)} %get-tuple-element.16.refs_1_, ...), custom_call_target="tpu_custom_call" | custom-call | tf_op jit(solution)/shard_map/hand_over/pallas_call | solution.py:545

commit v5 on v4

--- a/solution.py
+++ b/solution.py
@@ -49,9 +49,13 @@
     mom2,
     mixed,
     igrad,
+    out_p,
+    out_m,
+    out_v,
     new_p,
     new_m,
     new_v,
+    s_out,
     grads,
     scale_p,
     held_p,
@@ -397,11 +401,19 @@
 
     combine(0)
     combine(1)
+    written = []
+
+    def write(n, k):
+        src, dst = ((new_p, out_p), (new_m, out_m), (new_v, out_v))[n]
+        written.append(pltpu.make_async_copy(src.at[k], dst.at[k], s_out.at[n, k]))
+        written[-1].start()
+
     def second_moment(k):
         z_wait(2, k)
         grad = grads[k]
         v = beta_second * select(2, k).astype(F32) + (1.0 - beta_second) * grad * grad
         new_v[k] = v.astype(BF16)
+        write(2, k)
         root = jnp.sqrt(v * (1.0 / (1.0 - beta_second**adam_count)))
         scale_p[k] = (learn_rate / (1.0 - beta_first**adam_count)) / (root + adam_eps)
 
@@ -410,6 +422,8 @@
         m = beta_first * select(1, k).astype(F32) + (1.0 - beta_first) * grads[k]
         new_m[k] = m.astype(BF16)
         new_p[k] = (held_p[k].astype(F32) - m * scale_p[k]).astype(BF16)
+        write(1, k)
+        write(0, k)
 
     last = {}
     for t in range(half):
@@ -440,6 +454,8 @@
         out[...] = value.astype(BF16)
 
     first_moment(2)
+    for cp in written:
+        cp.wait()
 
     for cp in started:
         cp.wait_send()
@@ -476,6 +492,10 @@
     dma = pltpu.SemaphoreType.DMA
     pick = (half, NY * 2 * cap, 2 * tok_n)
     scratch = [
+        pltpu.VMEM(mat, BF16),
+        pltpu.VMEM(mat, BF16),
+        pltpu.VMEM(mat, BF16),
+        dma((3, 3)),
         pltpu.VMEM(mat, F32),
         pltpu.VMEM(mat, F32),
         pltpu.VMEM(mat, BF16),
@@ -525,7 +545,7 @@
             jax.ShapeDtypeStruct(mat, BF16),
         ),
         in_specs=[smem, smem, vmem, vmem] + [anywhere] * 5,
-        out_specs=(vmem,) * 5,
+        out_specs=(vmem,) * 2 + (anywhere,) * 3,
         scratch_shapes=scratch,
         compiler_params=pltpu.CompilerParams(
             collective_id=0, has_side_effects=True, vmem_limit_bytes=66 * 1000 * 1000

time: 226 us -> 226 us (level)
  no operation moved by 1% of the time
where the time goes in v5:
time: 226 us; the launch traced here: 225 us
  Pallas kernels  225 us (100%)
    pallas_call x1, Pallas kernels, on_device(): pl.pallas_call(functools.partial(kernel, nz, nx, cap), name='expert_step'...  222 us

profile of v5, /device:TPU:1, one launch (start us, length us, event | category | flops | bytes accessed | tf_op | source)
XLA Modules:
  0.0 225.5 jit_solution(5380969426761228264)
XLA Ops:
  0.6 222.4 %expert_step.1 = (bf16[128,256]{1,0:T(8,128)(2,1)}, bf16[128,256]{1,0:T(8,128)(2,1)}, bf16[3,256,384]{2,1,0:T(8,128)(2,1)}, bf16[3,256,384]{2,1,0:T(8,128)(2,1)}, bf16[3,256,384]{2,1,0:T(8,128)(2,1)}) custom-call(s32[64]{0:T(128)} %place.1, s32[2,64]{1,0:T(2,128)} %flags.1, s32[8,128]{1,0:T(8,128)} %bitcast.11, f32[8,128]{1,0:T(8,128)} %bitcast.12, ...), custom_call_target="tpu_custom_call" | custom-call | tf_op jit(solution)/shard_map/expert_step/pallas_call | solution.py:537
  223.0 2.4 %hand_over.1 = (bf16[128,256]{1,0:T(8,128)(2,1)}, bf16[128,256]{1,0:T(8,128)(2,1)}, bf16[3,256,384]{2,1,0:T(8,128)(2,1)}, bf16[3,256,384]{2,1,0:T(8,128)(2,1)}, bf16[3,256,384]{2,1,0:T(8,128)(2,1)}) custom-call(bf16[128,256]{1,0:T(8,128)(2,1)} %get-tuple-element.15.refs_0_, bf16[128,256]{1,0:T(8,128)(2,1)} %get-tuple-element.16.refs_1_, ...), custom_call_target="tpu_custom_call" | custom-call | tf_op jit(solution)/shard_map/hand_over/pallas_call | solution.py:565
